TPU v7x, 32 devices: a whole 2x2x4 slice. The times are simulated.
32 devices in a mesh: dp: 4 (over z), vocab: 8 (over y, x, core).
Axes of the slice: x: 2, y: 2, z: 4, core: 2. Of those that a mesh axis runs over, the one named last changes fastest.
Arguments:
- hidden: bfloat16 [4096, 4096], P(('dp', 'vocab')), may hold values from -4 to 4
- output_weight: bfloat16 [4096, 8192], P(None, 'vocab'), may hold values from -0.09375 to 0.09375
- owners: int32 [4096, 3], P(('dp', 'vocab')), may hold values from 0 to 7, all different within a row; in each aligned block of 128 rows (0 to 127, 128 to 255, ...) at most 64 rows name the same one
- negatives: int32 [4096, 3, 2], P(('dp', 'vocab')), may hold values from 0 to 7
- negative_mask: int32 [4096, 3, 2], P(('dp', 'vocab')), may hold values 0 or 1
- target_block: int32 [4096], P(('dp', 'vocab')), may hold values from 0 to 7
- target_word: int32 [4096], P(('dp', 'vocab')), may hold values from 0 to 127
- log_norm: bfloat16 [4096], P(('dp', 'vocab')), may hold values from 1 to 2
- cotangent: bfloat16 [4096], P(('dp', 'vocab')), may hold values from 4 to 8
Outputs:
- hidden_grad: bfloat16 [4096, 4096], P(('dp', 'vocab'))
- weight_grad: bfloat16 [4096, 8192], P('dp', 'vocab')
Inputs may be any that keep to these rules, and one draw needn't show every extreme that they name: Each row names 3 different owners; among the 128 rows of one device no owner is named by more than 64 rows, and in some device's rows an owner is named by exactly 64.
All inputs are finite; a program needn't handle non-finite values. No bound on the sum of `negative_mask` on one device may be relied on, other than what follows from the above.
Results may differ from a plain program's by a relative error of at most 0.015.
Values may be sent and summed in bfloat16 or wider, within the bound.
A program may use at most 128 MiB of HBM per device.

v0:
```python
import jax
import jax.numpy as jnp
from jax import lax
from jax.sharding import PartitionSpec as P

BLOCK = 128
BLK_DEV = 8
F32 = jnp.float32
BF16 = jnp.bfloat16


def body(
    hidden,
    output_weight,
    owners,
    negatives,
    negative_mask,
    target_block,
    target_word,
    log_norm,
    cotangent,
):
    tokens, width = hidden.shape
    visits = owners.shape[1]
    per_own = negatives.shape[2]
    n_vocab = lax.axis_size("vocab")
    n_dp = lax.axis_size("dp")
    me = lax.axis_index("vocab")
    my_dp = lax.axis_index("dp")
    words = output_weight.shape[1]
    capacity = max(2, tokens * visits * 4 // (3 * n_vocab))
    slots = n_vocab * capacity
    part = width // n_dp
    facts = jnp.concatenate(
        [
            owners.T,
            negatives.reshape(tokens, -1).T,
            negative_mask.reshape(tokens, -1).T,
            target_block[None, :],
            target_word[None, :],
        ],
        axis=0,
    ).astype(BF16)
    facts = jnp.concatenate([facts, log_norm[None, :], cotangent[None, :]], axis=0)
    facts = lax.all_gather(facts, ("dp", "vocab"), axis=0, tiled=False)
    blocks = n_dp * n_vocab
    group_rows = lax.all_gather(hidden, "vocab", axis=0, tiled=False)
    part_rows = lax.all_to_all(hidden, "dp", split_axis=1, concat_axis=0, tiled=True)
    part_rows = lax.all_gather(part_rows.reshape(n_dp, tokens, part), "vocab", axis=1)
    f = facts.astype(F32)
    pairs = visits * per_own
    hit = f[:, :visits, :] == me.astype(F32)
    neg = f[:, visits : visits + pairs, :]
    mask = f[:, visits + pairs : visits + 2 * pairs, :]
    base = visits + 2 * pairs
    t_block, t_word, norm, cot = (f[:, base + i, :] for i in range(4))
    named = jnp.any(hit, axis=1)
    cand = [jnp.where(hit[:, 0], t_block + 1.0, 0.0)]
    for n in range(per_own):
        value = jnp.zeros_like(t_block)
        for v in range(visits):
            i = v * per_own + n
            value = jnp.where(hit[:, v] & (mask[:, i] == 1.0), neg[:, i] + 1.0, value)
        cand.append(value)
    only = []
    for k, value in enumerate(cand):
        for earlier in cand[:k]:
            value = jnp.where(value == earlier, 0.0, value)
        only.append(value)
    upper = jnp.triu(jnp.ones((tokens, tokens), BF16), 1)
    rank = jnp.dot(named.astype(BF16), upper, preferred_element_type=F32)
    place = jnp.where(named, rank, -1.0)
    pick = (
        place[:, None, :] == jnp.arange(capacity, dtype=jnp.int32).astype(F32)[None, :, None]
    ).astype(BF16)
    attrs = jnp.stack(cand + only + [t_word, norm, cot], axis=1).astype(BF16)
    slot_facts = jnp.einsum("sct,sat->sca", pick, attrs, preferred_element_type=F32)
    kinds = per_own + 1
    all_only = slot_facts[:, :, kinds : 2 * kinds].reshape(n_dp * slots, kinds)
    mine = lax.dynamic_slice_in_dim(slot_facts, my_dp * n_vocab, n_vocab, 0).reshape(slots, -1)
    my_pick = lax.dynamic_slice_in_dim(pick, my_dp * n_vocab, n_vocab, 0)
    rows = jnp.einsum("sct,sth->sch", my_pick, group_rows, preferred_element_type=F32)
    rows = rows.astype(BF16).reshape(slots, width)
    scores = jnp.dot(rows, output_weight, preferred_element_type=F32)
    word_ids = jnp.arange(words, dtype=jnp.int32)[None, :]
    word_block = (word_ids // BLOCK + 1).astype(F32)
    word_in = (word_ids % BLOCK).astype(F32)
    counts = jnp.zeros((slots, words), F32)
    for k in range(kinds):
        counts = counts + jnp.where(mine[:, k : k + 1] == word_block, 1.0, 0.0)
    hot = jnp.where(
        (mine[:, 0:1] == word_block) & (mine[:, 2 * kinds : 2 * kinds + 1] == word_in), 1.0, 0.0
    )
    norm_col = mine[:, 2 * kinds + 1 : 2 * kinds + 2]
    cot_col = mine[:, 2 * kinds + 2 : 2 * kinds + 3]
    grown = jnp.where(counts > 0.0, counts * jnp.exp(scores - norm_col), 0.0)
    grad = (cot_col * (grown - hot)).astype(BF16)
    packed = []
    for k in range(kinds):
        which = mine[:, kinds + k : kinds + k + 1]
        value = jnp.zeros((slots, BLOCK), BF16)
        for b in range(BLK_DEV):
            value = jnp.where(which == b + 1.0, grad[:, b * BLOCK : (b + 1) * BLOCK], value)
        packed.append(value)
    packed = jnp.concatenate(packed, axis=1)
    packed = lax.all_gather(packed, "dp", axis=0, tiled=True)
    back = lax.dot_general(
        grad, output_weight, (((1,), (1,)), ((), ())), preferred_element_type=F32
    ).astype(BF16)
    back = jnp.einsum(
        "sct,sch->sth", my_pick, back.reshape(n_vocab, capacity, width), preferred_element_type=F32
    ).astype(BF16)
    hidden_grad = lax.psum_scatter(
        back.reshape(n_vocab * tokens, width), "vocab", scatter_dimension=0, tiled=True
    )
    part_slots = (
        jnp.einsum(
            "sct,sth->sch",
            pick,
            part_rows.reshape(blocks, tokens, part),
            preferred_element_type=F32,
        )
        .astype(BF16)
        .reshape(n_dp * slots, part)
    )
    spread = []
    for b in range(BLK_DEV):
        value = jnp.zeros((n_dp * slots, BLOCK), BF16)
        for k in range(kinds):
            value = jnp.where(
                all_only[:, k : k + 1] == b + 1.0, packed[:, k * BLOCK : (k + 1) * BLOCK], value
            )
        spread.append(value)
    spread = jnp.concatenate(spread, axis=1)
    weight_grad = lax.dot_general(
        part_slots, spread, (((0,), (0,)), ((), ())), preferred_element_type=F32
    ).astype(BF16)
    return (hidden_grad, weight_grad)


def solution(mesh):
    placed = (
        P(("dp", "vocab"), None),
        P(None, "vocab"),
        P(("dp", "vocab"), None),
        P(("dp", "vocab"), None, None),
        P(("dp", "vocab"), None, None),
        P(("dp", "vocab")),
        P(("dp", "vocab")),
        P(("dp", "vocab")),
        P(("dp", "vocab")),
    )
    return jax.shard_map(
        body,
        mesh=mesh,
        in_specs=placed,
        out_specs=(P(("dp", "vocab"), None), P("dp", "vocab")),
        check_vma=False,
    )
```

profile of v0, /device:TPU:0, one launch (start us, length us, event | category | flops | bytes accessed | tf_op | source)
XLA Modules:
  0.0 244.4 jit_solution(17321458530008942813)
XLA Ops:
  7.2 0.0 copy-start.2
  7.2 0.0 copy-start.3
  7.2 0.0 copy-start.5
  7.2 0.0 copy-start.6
  7.2 0.0 copy-start.4
  7.2 0.0 copy-start.7
  7.2 0.0 copy-start.8
  7.2 0.0 all-gather.10.cloned.1.call-start
  7.3 0.7 all-gather.10.cloned.1.call-update
  8.0 0.0 all-gather.12.cloned.1.call-start
  8.0 1.3 copy.20
  9.3 32.0 %all_to_all.16 = bf16[128,4,1024]{2,0,1:T(8,128)(2,1)} all-to-all(bf16[128,4,1024]{2,0,1:T(8,128)(2,1)S(1)} %bitcast.55), channel_id=1, replica_groups=mesh['dp'=4,'vocab'=8] {'dp'}, dimensions={1} | all-to-all | bytes 2097152 | tf_op jit(solution)/shard_map/all_to_all | solution.py:48
  41.3 0.0 all-gather.12.cloned.1.call-update
  41.3 0.0 all-gather.8.cloned.1.call-start
  41.4 0.0 copy-done.2
  41.4 0.0 copy-done.3
  41.5 0.0 copy-done.5
  41.5 0.0 copy-done.6
  41.5 0.0 copy-done.4
  41.5 0.0 copy-done.7
  41.5 0.0 copy-done.8
  41.5 0.2 concatenate.12
  41.7 40.7 %all-gather.3 = bf16[32,19,128]{2,1,0:T(8,128)(2,1)S(1)} all-gather(bf16[1,19,128]{2,1,0:T(8,128)(2,1)S(1)} %bitcast.56), channel_id=2, replica_groups=mesh['dp'=4,'vocab'=8] {'dp','vocab'}, dimensions={0}, use_global_device_ids=true | all-gather | bytes 160512 | tf_op jit(solution)/shard_map/all_gather | solution.py:45
  82.4 0.1 fusion.33
  82.5 0.3 fusion.17
  82.9 0.4 stack.4
  83.3 0.1 convolution_select_fusion
  83.4 0.5 fusion.3
  83.9 0.1 reshape.102
  84.0 0.1 compare_reduce_fusion.47
  84.2 0.2 broadcast_compare_fusion
  84.4 0.0 all-gather.10.cloned.1.call-done
  84.4 4.6 %convolution_convert_fusion.2 = bf16[8,64,4096]{2,1,0:T(8,128)(2,1)S(1)} fusion(bf16[8,128,4096]{2,1,0:T(8,128)(2,1)} %bitcast.48, pred[32,64,128]{2,1,0:T(32,128)(4,1)S(1)} %broadcast_compare_fusion, s32[]{:T(128)S(6)} %select_n.256), kind=kOutput, calls=%fused_computation.2 | convolution fusion | flops 538968064 | bytes 12648452 | tf_op jit(solution)/shard_map/sct,sth->sch/dot_general | solution.py:82
  89.1 8.7 %multiply_convert_fusion = bf16[512,1024]{1,0:T(8,128)(2,1)S(1)} fusion(bf16[512,4096]{1,0:T(8,128)(2,1)S(1)} %bitcast.49, bf16[4096,1024]{1,0:T(8,128)(2,1)} %param.10, f32[1024]{0:T(1024)S(1)} %get-tuple-element.78, f32[512]{0:T(512)S(1)} %bitcast.61, f32[1024]{0:T(1024)S(1)} %get-tuple-element.77, f32[512]{0:T(512)S(1)} %bitcast.64, f32[512]{0:T(512)S(1)} %bitcast.60, ...), kind=kOutput, calls=%fused_computation.8 | convolution fusion | flops 4304404480 | bytes 13651968 | tf_op jit(solution)/shard_map/dot_general | solution.py:84
  97.8 0.8 select_select_fusion
  98.5 0.8 select_select_fusion.1
  99.3 0.8 select_select_fusion.2
  100.1 0.8 pad_maximum_fusion
  100.9 0.0 all-gather.8.cloned.1.call-update
  100.9 0.2 reduce-scatter.2.cloned.1.call-start
  101.1 8.2 %convolution_convert_fusion.1 = bf16[512,4096]{1,0:T(8,128)(2,1)S(1)} fusion(bf16[512,1024]{1,0:T(8,128)(2,1)S(1)} %multiply_convert_fusion, bf16[4096,1024]{1,0:T(8,128)(2,1)} %param.10), kind=kOutput, calls=%fused_computation.1 | convolution fusion | flops 4297064448 | bytes 13631488 | tf_op jit(solution)/shard_map/dot_general | solution.py:107
  109.3 5.6 %convolution_convert_fusion = bf16[8,128,4096]{2,1,0:T(8,128)(2,1)} fusion(bf16[8,64,4096]{2,1,0:T(8,128)(2,1)S(1)} %bitcast.52, pred[32,64,128]{2,1,0:T(32,128)(4,1)S(1)} %broadcast_compare_fusion, s32[]{:T(128)S(6)} %select_n.256), kind=kOutput, calls=%fused_computation | convolution fusion | flops 541065216 | bytes 12648452 | tf_op jit(solution)/shard_map/sct,sch->sth/dot_general | solution.py:110
  114.9 0.0 reduce-scatter.2.cloned.1.call-update
  115.0 0.1 reshape.108
  115.1 0.6 compare_reduce_fusion.2
  115.7 8.7 %all-gather.12.cloned.1.call-done = bf16[4,1024,1024]{2,1,0:T(8,128)(2,1)} async-done(((bf16[4,128,1024]{2,1,0:T(8,128)(2,1)}), bf16[4,1024,1024]{2,1,0:T(8,128)(2,1)}) %all-gather.12.cloned.1.call-update) | async-done | bytes 8388624 | tf_op jit(solution)/shard_map/all_gather | solution.py:49
  124.4 6.6 %convolution_convert_fusion.3 = bf16[32,64,1024]{2,1,0:T(8,128)(2,1)} fusion(bf16[32,128,1024]{2,1,0:T(8,128)(2,1)} %bitcast.50, f32[32,128]{1,0:T(8,128)S(1)} %convolution_select_fusion, f32[64]{0:T(128)S(1)} %iota_convert_fusion), kind=kOutput, calls=%fused_computation.3 | convolution fusion | flops 539230208 | bytes 12599552 | tf_op jit(solution)/shard_map/sct,sth->sch/dot_general | solution.py:117
  131.0 32.6 %all-gather.8.cloned.1.call-done = bf16[2048,384]{1,0:T(8,128)(2,1)} async-done(((bf16[512,384]{1,0:T(8,128)(2,1)}), bf16[2048,384]{1,0:T(8,128)(2,1)}) %all-gather.8.cloned.1.call-update) | async-done | bytes 1572880 | tf_op jit(solution)/shard_map/all_gather | solution.py:106
  163.6 0.0 copy-start
  163.6 3.5 %select_dynamic-update-slice_fusion.7 = bf16[2048,1024]{1,0:T(8,128)(2,1)S(1)} fusion(pred[2048]{0:T(1024)(128)(4,1)S(1)} %get-tuple-element.58, pred[2048]{0:T(1024)(128)(4,1)S(1)} %get-tuple-element.57, pred[2048]{0:T(1024)(128)(4,1)S(1)} %get-tuple-element.56, bf16[2048,384]{1,0:T(8,128)(2,1)} %all-gather.8.cloned.1.call-done), kind=kLoop, calls=%fused_computation.22 | loop fusion | flops 786431 | bytes 2103296
  167.1 3.4 %select_dynamic-update-slice_fusion.6 = bf16[2048,1024]{1,0:T(8,128)(2,1)S(1)} fusion(bf16[2048,1024]{1,0:T(8,128)(2,1)S(1)} %select_dynamic-update-slice_fusion.7, pred[2048]{0:T(1024)(128)(4,1)S(1)} %get-tuple-element.16, pred[2048]{0:T(1024)(128)(4,1)S(1)} %get-tuple-element.9, pred[2048]{0:T(1024)(128)(4,1)S(1)} %get-tuple-element.3, ...), kind=kLoop, calls=%fused_computation.21 | loop fusion | flops 786432 | bytes 2103296
  170.5 0.0 copy-done
  170.5 1.8 select_dynamic-update-slice_fusion.5
  172.3 1.8 select_dynamic-update-slice_fusion.4
  174.1 0.0 copy-start.1
  174.1 1.8 select_dynamic-update-slice_fusion.3
  175.9 1.8 select_dynamic-update-slice_fusion.2
  177.6 1.8 select_dynamic-update-slice_fusion.1
  179.4 1.8 select_dynamic-update-slice_fusion
  181.2 0.0 copy-done.1
  181.2 5.7 %convolution_convert_fusion.4 = bf16[1024,1024]{1,0:T(8,128)(2,1)} fusion(bf16[2048,1024]{1,0:T(8,128)(2,1)S(1)} %bitcast.51, bf16[2048,1024]{1,0:T(8,128)(2,1)S(1)} %select_dynamic-update-slice_fusion), kind=kOutput, calls=%fused_computation.9 | convolution fusion | flops 4296015872 | bytes 10485760 | tf_op jit(solution)/shard_map/dot_general | solution.py:135
  187.0 50.9 %reduce-scatter.2.cloned.1.call-done = bf16[128,4096]{1,0:T(8,128)(2,1)} async-done(((bf16[1024,4096]{1,0:T(8,128)(2,1)}), bf16[128,4096]{1,0:T(8,128)(2,1)}) %reduce-scatter.2.cloned.1.call-update) | async-done | bytes 1048592 | tf_op jit(solution)/shard_map/reduce_scatter | solution.py:113
  (16 shorter events, 0.2 us)
Async XLA Ops:
  7.2 34.2 %copy-start.2 = (s32[128,3,2]{0,2,1:T(2,128)S(1)}, s32[128,3,2]{0,2,1:T(2,128)}, u32[]{:S(2)}) copy-start(s32[128,3,2]{0,2,1:T(2,128)} %param.12) | copy-start | bytes 9220
  7.2 34.3 %copy-start.3 = (s32[128,3,2]{0,2,1:T(2,128)S(1)}, s32[128,3,2]{0,2,1:T(2,128)}, u32[]{:S(2)}) copy-start(s32[128,3,2]{0,2,1:T(2,128)} %param.13) | copy-start | bytes 9220
  7.2 34.3 %copy-start.5 = (s32[128]{0:T(128)S(1)}, s32[128]{0:T(128)}, u32[]{:S(2)}) copy-start(s32[128]{0:T(128)} %param.15) | copy-start | bytes 1540
  7.2 34.3 %copy-start.6 = (s32[128]{0:T(128)S(1)}, s32[128]{0:T(128)}, u32[]{:S(2)}) copy-start(s32[128]{0:T(128)} %param.14) | copy-start | bytes 1540
  7.2 34.3 %copy-start.4 = (s32[128,3]{0,1:T(4,128)S(1)}, s32[128,3]{0,1:T(4,128)}, u32[]{:S(2)}) copy-start(s32[128,3]{0,1:T(4,128)} %param.11) | copy-start | bytes 4612
  7.2 34.3 %copy-start.7 = (bf16[128]{0:T(256)(128)(2,1)S(1)}, bf16[128]{0:T(256)(128)(2,1)}, u32[]{:S(2)}) copy-start(bf16[128]{0:T(256)(128)(2,1)} %param.16) | copy-start | bytes 772
  7.2 34.3 %copy-start.8 = (bf16[128]{0:T(256)(128)(2,1)S(1)}, bf16[128]{0:T(256)(128)(2,1)}, u32[]{:S(2)}) copy-start(bf16[128]{0:T(256)(128)(2,1)} %param.17) | copy-start | bytes 772
  7.2 77.2 %all-gather.10.cloned.1.call-start = ((), (), s32[]{:S(2)}) async-start(), calls=%async_computation.4 | async-start | bytes 9437184 | tf_op jit(solution)/shard_map/all_gather | solution.py:47
  8.0 116.4 %all-gather.12.cloned.1.call-start = ((), (), s32[]{:S(2)}) async-start(), calls=%async_computation.5 | async-start | bytes 9437184 | tf_op jit(solution)/shard_map/all_gather | solution.py:49
  41.3 122.3 %all-gather.8.cloned.1.call-start = ((), (), s32[]{:S(2)}) async-start(), calls=%async_computation.3 | async-start | bytes 1966080 | tf_op jit(solution)/shard_map/all_gather | solution.py:106
  100.9 137.0 %reduce-scatter.2.cloned.1.call-start = ((), (), s32[]{:S(2)}) async-start(), calls=%async_computation.2 | async-start | bytes 9437184 | tf_op jit(solution)/shard_map/reduce_scatter | solution.py:113
  163.6 6.9 %copy-start = (bf16[2048,384]{1,0:T(8,128)(2,1)S(1)}, bf16[2048,384]{1,0:T(8,128)(2,1)}, u32[]{:S(2)}) copy-start(bf16[2048,384]{1,0:T(8,128)(2,1)} %all-gather.8.cloned.1.call-done) | copy-start | bytes 4718596
  174.1 7.1 %copy-start.1 = (bf16[32,64,1024]{2,1,0:T(8,128)(2,1)S(1)}, bf16[32,64,1024]{2,1,0:T(8,128)(2,1)}, u32[]{:S(2)}) copy-start(bf16[32,64,1024]{2,1,0:T(8,128)(2,1)} %convolution_convert_fusion.3) | copy-start | bytes 12582916
Sparse Core Ops, SparseCore 0:
  9.9 58.0 all-gather.9
  70.0 54.3 all-gather.11
  126.5 37.0 all-gather.7
  167.5 70.3 reduce-scatter.1
where the time goes:
time: 245 us; the launch traced here: 244 us
  waiting for transfers between devices  93 us (38%)
  blocking collectives  72.6 us (30%)
  matrix products  40 us (16%)
  other arithmetic  22 us (9%)
  between operations  14.2 us (6%)
    reduce_scatter x1, waiting for transfers between devices, body(): lax.psum_scatter(back.reshape(n_vocab * tokens, width), 'vocab', scatter_...  50.9 us
    all_gather x1, blocking collectives, body(): facts = lax.all_gather(facts, ('dp', 'vocab'), axis=0, tiled=False)  40.7 us
    all_gather x1, waiting for transfers between devices, body(): packed = lax.all_gather(packed, 'dp', axis=0, tiled=True)  32.6 us
    all_to_all x1, blocking collectives, body(): lax.all_to_all(hidden, 'dp', split_axis=1, concat_axis=0, tiled=True)  32 us
    unnamed x7, other arithmetic  15.7 us
    all_gather x1, waiting for transfers between devices, body(): lax.all_gather(part_rows.reshape(n_dp, tokens, part), 'vocab', axis=1)  8.72 us
    dot_general x1, matrix products, body(): scores = jnp.dot(rows, output_weight, preferred_element_type=F32)  8.7 us
    dot_general x1, matrix products, body(): lax.dot_general(grad, output_weight, (((1,), (1,)), ((), ())), preferred_...  8.19 us
  transfers between devices with their start and end apart: 4, of which 3 were waited for; matrix products, arithmetic and copies ran while one was open for 26% of the time, Pallas kernels for 0%

commit v1 on v0

--- a/solution.py
+++ b/solution.py
@@ -1,3 +1,4 @@
+import functools
 import jax
 import jax.numpy as jnp
 from jax import lax
@@ -7,6 +8,25 @@
 BLK_DEV = 8
 F32 = jnp.float32
 BF16 = jnp.bfloat16
+
+
+def play_the_block(content, comm_axis, pos_dim):
+    n_parts = lax.axis_size(comm_axis)
+    u1 = [(ix - 1, ix) for ix in range(1, n_parts)] + [(n_parts - 1, 0)]
+    view_out = content
+    frames = [view_out]
+    for _ in range(n_parts - 1):
+        view_out = lax.ppermute(view_out, comm_axis, u1)
+        frames += [view_out]
+    after = jnp.roll(
+        jnp.concatenate([*reversed(frames)], axis=pos_dim),
+        (lax.axis_index(comm_axis) + 1) * view_out.shape[pos_dim],
+        pos_dim,
+    )
+    return after
+
+
+quotas_extend = functools.partial(play_the_block, comm_axis="dp", pos_dim=0)
 
 
 def body(
@@ -103,7 +123,7 @@
             value = jnp.where(which == b + 1.0, grad[:, b * BLOCK : (b + 1) * BLOCK], value)
         packed.append(value)
     packed = jnp.concatenate(packed, axis=1)
-    packed = lax.all_gather(packed, "dp", axis=0, tiled=True)
+    packed = quotas_extend(packed)
     back = lax.dot_general(
         grad, output_weight, (((1,), (1,)), ((), ())), preferred_element_type=F32
     ).astype(BF16)

time: 245 us -> 207 us (0.84)
  waiting for transfers between devices: 93 us -> 42.6 us
  other arithmetic: 22 us -> 37 us
  matrix products: 40 us -> 37.3 us
    reduce_scatter x1, waiting for transfers between devices: 50.9 us -> 5.71 us  [body(): lax.psum_scatter(back.reshape(n_vocab * tokens, width), 'vocab', scatter_...]
    ppermute x0 -> x3, waiting for transfers between devices: none -> 36.2 us  [play_the_block(): view_out = lax.ppermute(view_out, comm_axis, u1)]
    all_gather x1 -> x0, waiting for transfers between devices: 32.6 us -> none  [body(): packed = lax.all_gather(packed, 'dp', axis=0, tiled=True)]
    unnamed x7 -> x9, other arithmetic: 15.7 us -> 28.9 us
    all_gather x1, waiting for transfers between devices: 8.72 us -> 0.01 us  [body(): lax.all_gather(part_rows.reshape(n_dp, tokens, part), 'vocab', axis=1)]
    dot_general x1, matrix products: 8.19 us -> 4.8 us  [body(): lax.dot_general(grad, output_weight, (((1,), (1,)), ((), ())), preferred_...]
    concatenate x1, other arithmetic: 1.77 us -> 4.25 us  [body(): spread = jnp.concatenate(spread, axis=1)]
  transfers between devices with their start and end apart: 4 -> 6, of which waited for: 3 -> 4; matrix products, arithmetic and copies ran while one was open for 26% -> 37% of each run, Pallas kernels for 0% -> 0%
where the time goes in v1:
time: 207 us; the launch traced here: 206 us
  blocking collectives  72.6 us (35%)
  waiting for transfers between devices  42.6 us (21%)
  matrix products  37.3 us (18%)
  other arithmetic  37 us (18%)
  between operations  14.2 us (7%)
  local copies, waits for them, and re-layouts  2.55 us (1%)
    all_gather x1, blocking collectives, body(): facts = lax.all_gather(facts, ('dp', 'vocab'), axis=0, tiled=False)  40.7 us
    ppermute x3, waiting for transfers between devices, play_the_block(): view_out = lax.ppermute(view_out, comm_axis, u1)  36.2 us
    all_to_all x1, blocking collectives, body(): lax.all_to_all(hidden, 'dp', split_axis=1, concat_axis=0, tiled=True)  32 us
    unnamed x9, other arithmetic  28.9 us
    dot_general x1, matrix products, body(): scores = jnp.dot(rows, output_weight, preferred_element_type=F32)  8.85 us
    dot_general x1, matrix products, body(): lax.dot_general(part_slots, spread, (((0,), (0,)), ((), ())), preferred_e...  7.99 us
    reduce_scatter x1, waiting for transfers between devices, body(): lax.psum_scatter(back.reshape(n_vocab * tokens, width), 'vocab', scatter_...  5.71 us
    dot_general x1, matrix products, body(): jnp.einsum('sct,sch->sth', my_pick, back.reshape(n_vocab, capacity, width...  5.59 us
  transfers between devices with their start and end apart: 6, of which 4 were waited for; matrix products, arithmetic and copies ran while one was open for 37% of the time, Pallas kernels for 0%

profile of v1, /device:TPU:0, one launch (start us, length us, event | category | flops | bytes accessed | tf_op | source)
XLA Modules:
  0.0 206.5 jit_solution(4912916859288794732)
XLA Ops:
  7.2 0.0 copy-start.1
  7.2 0.0 copy-start.2
  7.2 0.0 copy-start.4
  7.2 0.0 copy-start.5
  7.2 0.0 copy-start.3
  7.2 0.0 copy-start.6
  7.2 0.0 all-gather.7.cloned.1.call-start
  7.3 0.7 all-gather.7.cloned.1.call-update
  8.0 0.0 all-gather.9.cloned.1.call-start
  8.0 1.3 copy.20
  9.3 32.0 %all_to_all.16 = bf16[128,4,1024]{2,0,1:T(8,128)(2,1)} all-to-all(bf16[128,4,1024]{2,0,1:T(8,128)(2,1)S(1)} %bitcast.55), channel_id=1, replica_groups=mesh['dp'=4,'vocab'=8] {'dp'}, dimensions={1} | all-to-all | bytes 2097152 | tf_op jit(solution)/shard_map/all_to_all | solution.py:68
  41.3 0.0 all-gather.9.cloned.1.call-update
  41.3 0.0 reduce-scatter.2.cloned.1.call-start
  41.5 0.0 copy-done.5
  41.5 0.0 copy-done.6
  41.5 0.0 copy-done.7
  41.5 0.2 concatenate.18
  41.7 40.7 %all-gather.3 = bf16[32,19,128]{2,1,0:T(8,128)(2,1)S(1)} all-gather(bf16[1,19,128]{2,1,0:T(8,128)(2,1)S(1)} %bitcast.56), channel_id=2, replica_groups=mesh['dp'=4,'vocab'=8] {'dp','vocab'}, dimensions={0}, use_global_device_ids=true | all-gather | bytes 160512 | tf_op jit(solution)/shard_map/all_gather | solution.py:65
  82.4 0.1 fusion.33
  82.5 0.3 fusion.17
  82.9 0.4 stack.4
  83.3 0.1 convolution_select_fusion
  83.4 0.5 fusion.3
  83.9 0.1 reshape.102
  84.0 0.2 broadcast_compare_fusion
  84.2 0.0 all-gather.7.cloned.1.call-done
  84.3 0.0 slice-start
  84.3 4.8 %convolution_convert_fusion.2 = bf16[8,64,4096]{2,1,0:T(8,128)(2,1)S(1)} fusion(bf16[8,128,4096]{2,1,0:T(8,128)(2,1)} %bitcast.48, pred[32,64,128]{2,1,0:T(32,128)(4,1)S(1)} %broadcast_compare_fusion, s32[]{:T(128)S(6)} %select_n.268), kind=kOutput, calls=%fused_computation.2 | convolution fusion | flops 538968064 | bytes 12648452 | tf_op jit(solution)/shard_map/sct,sth->sch/dot_general | solution.py:102
  89.1 0.0 slice-start.1
  89.1 8.8 %multiply_convert_fusion = bf16[512,1024]{1,0:T(8,128)(2,1)S(1)} fusion(bf16[512,4096]{1,0:T(8,128)(2,1)S(1)} %bitcast.49, bf16[4096,1024]{1,0:T(8,128)(2,1)} %param.10, f32[1024]{0:T(1024)S(1)} %get-tuple-element.78, f32[512]{0:T(512)S(1)} %bitcast.61, f32[1024]{0:T(1024)S(1)} %get-tuple-element.77, f32[512]{0:T(512)S(1)} %bitcast.64, f32[512]{0:T(512)S(1)} %bitcast.60, ...), kind=kOutput, calls=%fused_computation.8 | convolution fusion | flops 4304404480 | bytes 13651968 | tf_op jit(solution)/shard_map/dot_general | solution.py:104
  98.0 4.8 %convolution_convert_fusion.1 = bf16[512,4096]{1,0:T(8,128)(2,1)S(1)} fusion(bf16[512,1024]{1,0:T(8,128)(2,1)S(1)} %multiply_convert_fusion, bf16[4096,1024]{1,0:T(8,128)(2,1)S(1)} %bitcast.68), kind=kOutput, calls=%fused_computation.1 | convolution fusion | flops 4297064448 | bytes 13631488 | tf_op jit(solution)/shard_map/dot_general | solution.py:127
  102.8 5.6 %convolution_convert_fusion = bf16[8,128,4096]{2,1,0:T(8,128)(2,1)} fusion(bf16[8,64,4096]{2,1,0:T(8,128)(2,1)S(1)} %bitcast.52, pred[32,64,128]{2,1,0:T(32,128)(4,1)S(1)} %broadcast_compare_fusion, s32[]{:T(128)S(6)} %select_n.268), kind=kOutput, calls=%fused_computation | convolution fusion | flops 541065216 | bytes 12648452 | tf_op jit(solution)/shard_map/sct,sch->sth/dot_general | solution.py:130
  108.4 0.0 reduce-scatter.2.cloned.1.call-update
  108.4 0.2 compare_reduce_fusion.47
  108.5 0.8 select_select_fusion
  109.3 0.8 select_select_fusion.1
  110.1 0.8 select_select_fusion.2
  110.9 0.1 pad_maximum_fusion
  110.9 0.1 collective-permute-start
  111.0 13.1 %collective-permute-done = bf16[512,384]{1,0:T(8,128)(2,1)S(1)} collective-permute-done((bf16[512,384]{1,0:T(8,128)(2,1)S(1)}, bf16[512,384]{1,0:T(8,128)(2,1)S(1)}, u32[]{:S(2)}, u32[]{:S(2)}) %collective-permute-start) | collective-permute-done | bytes 393248 | tf_op jit(solution)/shard_map/ppermute | solution.py:19
  124.1 0.0 collective-permute-start.1
  124.1 12.3 %collective-permute-done.1 = bf16[512,384]{1,0:T(8,128)(2,1)S(1)} collective-permute-done((bf16[512,384]{1,0:T(8,128)(2,1)S(1)}, bf16[512,384]{1,0:T(8,128)(2,1)S(1)}, u32[]{:S(2)}, u32[]{:S(2)}) %collective-permute-start.1) | collective-permute-done | bytes 393248 | tf_op jit(solution)/shard_map/ppermute | solution.py:19
  136.4 0.0 collective-permute-start.2
  136.5 0.1 reshape.108
  136.6 0.6 compare_reduce_fusion.2
  137.2 10.7 %collective-permute-done.2 = bf16[512,384]{1,0:T(8,128)(2,1)S(1)} collective-permute-done((bf16[512,384]{1,0:T(8,128)(2,1)S(1)}, bf16[512,384]{1,0:T(8,128)(2,1)S(1)}, u32[]{:S(2)}, u32[]{:S(2)}) %collective-permute-start.2) | collective-permute-done | bytes 393248 | tf_op jit(solution)/shard_map/ppermute | solution.py:19
  147.9 0.1 constant_dynamic-update-slice_fusion.6
  148.0 0.1 constant_dynamic-update-slice_fusion.5
  148.1 0.1 constant_dynamic-update-slice_fusion.4
  148.2 0.1 constant_dynamic-update-slice_fusion.3
  148.2 0.1 constant_dynamic-update-slice_fusion.2
  148.3 0.1 constant_dynamic-update-slice_fusion.1
  148.4 0.1 constant_dynamic-update-slice_fusion
  148.5 3.0 %select_dynamic-update-slice_fusion.7 = bf16[2048,1024]{1,0:T(8,128)(2,1)} fusion(pred[2048]{0:T(1024)(128)(4,1)S(1)} %get-tuple-element.58, pred[2048]{0:T(1024)(128)(4,1)S(1)} %get-tuple-element.57, pred[2048]{0:T(1024)(128)(4,1)S(1)} %get-tuple-element.56, bf16[4096,384]{1,0:T(8,128)(2,1)S(1)} %constant_dynamic-update-slice_fusion, s32[]{:T(128)S(6)} %select_n.311, ...), kind=kLoop, calls=%fused_computation.22 | loop fusion | flops 786431 | bytes 2103308
  151.5 4.4 %select_dynamic-update-slice_fusion.6 = bf16[2048,1024]{1,0:T(8,128)(2,1)} fusion(bf16[2048,1024]{1,0:T(8,128)(2,1)} %select_dynamic-update-slice_fusion.7, pred[2048]{0:T(1024)(128)(4,1)S(1)} %get-tuple-element.16, pred[2048]{0:T(1024)(128)(4,1)S(1)} %get-tuple-element.9, pred[2048]{0:T(1024)(128)(4,1)S(1)} %get-tuple-element.3, ...), kind=kLoop, calls=%fused_computation.21 | loop fusion | flops 786432 | bytes 2103308
  155.9 4.2 %select_dynamic-update-slice_fusion.5 = bf16[2048,1024]{1,0:T(8,128)(2,1)} fusion(bf16[2048,1024]{1,0:T(8,128)(2,1)} %select_dynamic-update-slice_fusion.6, pred[2048]{0:T(1024)(128)(4,1)S(1)} %get-tuple-element.17, pred[2048]{0:T(1024)(128)(4,1)S(1)} %get-tuple-element.10, pred[2048]{0:T(1024)(128)(4,1)S(1)} %get-tuple-element.4, ...), kind=kLoop, calls=%fused_computation.20 | loop fusion | flops 786432 | bytes 2103308
  160.1 4.4 %select_dynamic-update-slice_fusion.4 = bf16[2048,1024]{1,0:T(8,128)(2,1)} fusion(bf16[2048,1024]{1,0:T(8,128)(2,1)} %select_dynamic-update-slice_fusion.5, pred[2048]{0:T(1024)(128)(4,1)S(1)} %get-tuple-element.18, pred[2048]{0:T(1024)(128)(4,1)S(1)} %get-tuple-element.11, pred[2048]{0:T(1024)(128)(4,1)S(1)} %get-tuple-element.5, ...), kind=kLoop, calls=%fused_computation.19 | loop fusion | flops 786432 | bytes 2103308
  164.5 4.2 %select_dynamic-update-slice_fusion.3 = bf16[2048,1024]{1,0:T(8,128)(2,1)} fusion(bf16[2048,1024]{1,0:T(8,128)(2,1)} %select_dynamic-update-slice_fusion.4, pred[2048]{0:T(1024)(128)(4,1)S(1)} %get-tuple-element.19, pred[2048]{0:T(1024)(128)(4,1)S(1)} %get-tuple-element.12, pred[2048]{0:T(1024)(128)(4,1)S(1)} %get-tuple-element.6, ...), kind=kLoop, calls=%fused_computation.18 | loop fusion | flops 786432 | bytes 2103308
  168.7 4.3 %select_dynamic-update-slice_fusion.2 = bf16[2048,1024]{1,0:T(8,128)(2,1)} fusion(bf16[2048,1024]{1,0:T(8,128)(2,1)} %select_dynamic-update-slice_fusion.3, pred[2048]{0:T(1024)(128)(4,1)S(1)} %get-tuple-element.20, pred[2048]{0:T(1024)(128)(4,1)S(1)} %get-tuple-element.13, pred[2048]{0:T(1024)(128)(4,1)S(1)} %get-tuple-element.7, ...), kind=kLoop, calls=%fused_computation.17 | loop fusion | flops 786432 | bytes 2103308
  173.1 4.3 %select_dynamic-update-slice_fusion.1 = bf16[2048,1024]{1,0:T(8,128)(2,1)} fusion(bf16[2048,1024]{1,0:T(8,128)(2,1)} %select_dynamic-update-slice_fusion.2, pred[2048]{0:T(1024)(128)(4,1)S(1)} %get-tuple-element.59, pred[2048]{0:T(1024)(128)(4,1)S(1)} %get-tuple-element.14, pred[2048]{0:T(1024)(128)(4,1)S(1)} %get-tuple-element.8, ...), kind=kLoop, calls=%fused_computation.16 | loop fusion | flops 786432 | bytes 2103308
  177.3 4.2 %select_dynamic-update-slice_fusion = bf16[2048,1024]{1,0:T(8,128)(2,1)} fusion(bf16[2048,1024]{1,0:T(8,128)(2,1)} %select_dynamic-update-slice_fusion.1, pred[2048]{0:T(1024)(128)(4,1)S(1)} %get-tuple-element.60, pred[2048]{0:T(1024)(128)(4,1)S(1)} %get-tuple-element.15, pred[2048]{0:T(1024)(128)(4,1)S(1)} %get-tuple-element.2, ...), kind=kLoop, calls=%fused_computation.15 | loop fusion | flops 786432 | bytes 2103308 | tf_op jit(solution)/shard_map/concatenate | solution.py:154
  181.6 4.7 %convolution_convert_fusion.3 = bf16[32,64,1024]{2,1,0:T(8,128)(2,1)S(1)} fusion(bf16[32,128,1024]{2,1,0:T(8,128)(2,1)} %bitcast.50, f32[32,128]{1,0:T(8,128)S(1)} %convolution_select_fusion, f32[64]{0:T(128)S(1)} %iota_convert_fusion), kind=kOutput, calls=%fused_computation.3 | convolution fusion | flops 539230208 | bytes 12599552 | tf_op jit(solution)/shard_map/sct,sth->sch/dot_general | solution.py:137
  186.3 8.0 %convolution_convert_fusion.4 = bf16[1024,1024]{1,0:T(8,128)(2,1)} fusion(bf16[2048,1024]{1,0:T(8,128)(2,1)S(1)} %bitcast.51, bf16[2048,1024]{1,0:T(8,128)(2,1)} %select_dynamic-update-slice_fusion), kind=kOutput, calls=%fused_computation.9 | convolution fusion | flops 4296015872 | bytes 10485760 | tf_op jit(solution)/shard_map/dot_general | solution.py:155
  194.2 5.7 %reduce-scatter.2.cloned.1.call-done = bf16[128,4096]{1,0:T(8,128)(2,1)} async-done(((bf16[1024,4096]{1,0:T(8,128)(2,1)}), bf16[128,4096]{1,0:T(8,128)(2,1)}) %reduce-scatter.2.cloned.1.call-update) | async-done | bytes 1048592 | tf_op jit(solution)/shard_map/reduce_scatter | solution.py:133
  (28 shorter events, 0.3 us)
Async XLA Ops:
  7.2 34.2 %copy-start.1 = (s32[128,3,2]{0,2,1:T(2,128)S(1)}, s32[128,3,2]{0,2,1:T(2,128)}, u32[]{:S(2)}) copy-start(s32[128,3,2]{0,2,1:T(2,128)} %param.12) | copy-start | bytes 9220
  7.2 34.3 %copy-start.2 = (s32[128,3,2]{0,2,1:T(2,128)S(1)}, s32[128,3,2]{0,2,1:T(2,128)}, u32[]{:S(2)}) copy-start(s32[128,3,2]{0,2,1:T(2,128)} %param.13) | copy-start | bytes 9220
  7.2 34.3 %copy-start.4 = (s32[128]{0:T(128)S(1)}, s32[128]{0:T(128)}, u32[]{:S(2)}) copy-start(s32[128]{0:T(128)} %param.15) | copy-start | bytes 1540
  7.2 34.3 %copy-start.5 = (s32[128]{0:T(128)S(1)}, s32[128]{0:T(128)}, u32[]{:S(2)}) copy-start(s32[128]{0:T(128)} %param.14) | copy-start | bytes 1540
  7.2 34.3 %copy-start.3 = (s32[128,3]{0,1:T(4,128)S(1)}, s32[128,3]{0,1:T(4,128)}, u32[]{:S(2)}) copy-start(s32[128,3]{0,1:T(4,128)} %param.11) | copy-start | bytes 4612
  7.2 34.3 %copy-start.6 = (bf16[128]{0:T(256)(128)(2,1)S(1)}, bf16[128]{0:T(256)(128)(2,1)}, u32[]{:S(2)}) copy-start(bf16[128]{0:T(256)(128)(2,1)} %param.16) | copy-start | bytes 772
  7.2 34.3 %copy-start.7 = (bf16[128]{0:T(256)(128)(2,1)S(1)}, bf16[128]{0:T(256)(128)(2,1)}, u32[]{:S(2)}) copy-start(bf16[128]{0:T(256)(128)(2,1)} %param.17) | copy-start | bytes 772
  7.2 77.0 %all-gather.7.cloned.1.call-start = ((), (), s32[]{:S(2)}) async-start(), calls=%async_computation.3 | async-start | bytes 9437184 | tf_op jit(solution)/shard_map/all_gather | solution.py:67
  8.0 173.6 %all-gather.9.cloned.1.call-start = ((), (), s32[]{:S(2)}) async-start(), calls=%async_computation.4 | async-start | bytes 9437184 | tf_op jit(solution)/shard_map/all_gather | solution.py:69
  41.3 158.6 %reduce-scatter.2.cloned.1.call-start = ((), (), s32[]{:S(2)}) async-start(), calls=%async_computation.2 | async-start | bytes 9437184 | tf_op jit(solution)/shard_map/reduce_scatter | solution.py:133
  84.3 13.7 %slice-start = ((s8[8388608]{0:T(1024)(128)(4,1)}), s8[4194304]{0:T(1024)(128)(4,1)S(1)}, s32[]{:S(2)}) async-start(s8[8388608]{0:T(1024)(128)(4,1)} %bitcast.67), calls=%async_computation.5 | async-start | bytes 8388608
  89.1 8.9 %slice-start.1 = ((s8[8388608]{0:T(1024)(128)(4,1)}), s8[4194304]{0:T(1024)(128)(4,1)S(1)}, s32[]{:S(2)}) async-start(s8[8388608]{0:T(1024)(128)(4,1)} %bitcast.67), calls=%async_computation.6 | async-start | bytes 8388608
  110.9 13.2 %collective-permute-start = (bf16[512,384]{1,0:T(8,128)(2,1)S(1)}, bf16[512,384]{1,0:T(8,128)(2,1)S(1)}, u32[]{:S(2)}, u32[]{:S(2)}) collective-permute-start(bf16[512,384]{1,0:T(8,128)(2,1)S(1)} %pad_maximum_fusion), channel_id=1, source_target_pairs={{0,8},{8,16},{16,24},{24,0},{1,9},{9,17},{17,25},{25,1},{2,10},{10... | collective-permute-start | bytes 1179656 | tf_op jit(solution)/shard_map/ppermute | solution.py:19
  124.1 12.3 %collective-permute-start.1 = (bf16[512,384]{1,0:T(8,128)(2,1)S(1)}, bf16[512,384]{1,0:T(8,128)(2,1)S(1)}, u32[]{:S(2)}, u32[]{:S(2)}) collective-permute-start(bf16[512,384]{1,0:T(8,128)(2,1)S(1)} %collective-permute-done), channel_id=1, source_target_pairs={{0,8},{8,16},{16,24},{24,0},{1,9},{9,17},{17,25},{25,1},{2,10},{10... | collective-permute-start | bytes 1179656 | tf_op jit(solution)/shard_map/ppermute | solution.py:19
  136.4 11.4 %collective-permute-start.2 = (bf16[512,384]{1,0:T(8,128)(2,1)S(1)}, bf16[512,384]{1,0:T(8,128)(2,1)S(1)}, u32[]{:S(2)}, u32[]{:S(2)}) collective-permute-start(bf16[512,384]{1,0:T(8,128)(2,1)S(1)} %collective-permute-done.1), channel_id=1, source_target_pairs={{0,8},{8,16},{16,24},{24,0},{1,9},{9,17},{17,25},{25,1},{2,10},{10... | collective-permute-start | bytes 1179656 | tf_op jit(solution)/shard_map/ppermute | solution.py:19
  148.5 3.0 %copy-start = (bf16[4096,384]{1,0:T(8,128)(2,1)}, bf16[4096,384]{1,0:T(8,128)(2,1)S(1)}, u32[]{:S(2)}) copy-start(bf16[4096,384]{1,0:T(8,128)(2,1)S(1)} %constant_dynamic-update-slice_fusion) | copy-start | bytes 9437188
Sparse Core Ops, SparseCore 0:
  9.9 58.0 all-gather.6
  70.0 54.3 all-gather.8
  128.4 71.4 reduce-scatter.1
